TPU v7x, 256 devices: a whole 4x4x8 slice. The times are simulated.
256 devices in a mesh: tiles: 64 (over y, x_lo, z), probes: 4 (over x_hi, core).
Axes of the slice: x: 4 (x_hi: 2, x_lo: 2; x = x_hi * 2 + x_lo), y: 4, z: 8, core: 2. Of those that a mesh axis runs over, the one named last changes fastest.
Arguments:
- blocks: bfloat16 [4096, 192, 192], P('tiles'), may hold values from -0.21875 to 0.21875
- connectivity: int32 [4096, 64], P('tiles'), may hold values from 0 to 4607, as said below
- basal_map: int32 [4096, 64], P('tiles'), may hold values from 0 to 383
- friction: float32 [4096, 64, 3], P('tiles'), may hold values from 0.2 to 2
- elem_counts: int32 [64], P('tiles'), may hold values from 1 to 64, 3072 in all
- obs_weight: float32 [262144, 3], P('tiles'), may hold values from 0.2 to 2
- sign_bits: int32 [16384, 32], P('tiles', 'probes'), may hold values from 0 to 1
- cluster_ids: int32 [16384], P('tiles'), may hold values from 0 to 63, never falling along the last dimension, each value on 1 to 512 neighbouring positions
Outputs:
- samples: float32 [16384, 32], P('tiles', 'probes')
- refined: float32 [16384, 32], P('tiles', 'probes')
- gram: float32 [64, 32, 32], P(None, 'probes')
Inputs may be any that keep to these rules, and one draw needn't show every extreme that they name: `connectivity`: about one reference in eight names a node of the next tile. `elem_counts`: some tile has all 64 slots live. `cluster_ids`: never falling along the cells; each cluster holds 1 to 512 cells.
All inputs are finite; a program needn't handle non-finite values. No bound on the sum of `elem_counts` on one device may be relied on, other than what follows from the above.
Results may differ from a plain program's by a relative error of at most 0.004.
Values may be sent and summed in bfloat16 or wider, within the bound.
A program may use at most 64 MiB of HBM per device.

v0:
```python
import jax
import jax.numpy as jnp
from jax import lax
from jax.sharding import PartitionSpec as P

HALO = 512
POWER = 2
RIM = 64


def padded(x, sides, width):
    for axis, dim in sides:
        size, length = (lax.axis_size(axis), x.shape[dim])
        up = [(i, (i + 1) % size) for i in range(size - 1)]
        down = [(j, i) for i, j in up]
        last = lax.slice_in_dim(x, length - width, length, axis=dim)
        leading = lax.slice_in_dim(x, 0, width, axis=dim)
        before = lax.ppermute(last, axis, up)
        after = lax.ppermute(leading, axis, down)
        x = jnp.concatenate([before, x, after], axis=dim)
    return x


def from_behind(block, axis, distance):
    devices = range(lax.axis_size(axis))
    route = [(i - distance, i) for i in devices if i - distance in devices]
    return lax.ppermute(block, axis, route)


def shards(
    blocks, connectivity, basal_map, friction, elem_counts, obs_weight, sign_bits, cluster_ids
):
    elem_slots = blocks.shape[0]
    block_order = blocks.shape[1]
    node_slots = connectivity.shape[1]
    node_count = obs_weight.shape[0]
    halo_nodes = HALO
    rim_cells = RIM
    cell_count = sign_bits.shape[0]
    group_size = sign_bits.shape[1]
    tile_count = lax.axis_size("tiles")
    alive_slots = jnp.arange(elem_slots, dtype=jnp.int32) < elem_counts[0]
    flat_nodes = connectivity.reshape(-1)
    flat_cells = basal_map.reshape(-1)

    def hessian(probe_field):
        window = padded(probe_field, (("tiles", 0),), rim_cells)
        picked = window[basal_map]
        inputs = (friction[:, :, :, None] * picked[:, :, None, :]).astype(jnp.bfloat16)
        inputs = inputs.reshape(elem_slots, block_order, group_size)
        forward = jnp.einsum("eij,ejp->eip", blocks, inputs, preferred_element_type=jnp.float32)
        forward = jnp.where(alive_slots[:, None, None], forward, jnp.float32(0.0))
        summed = jax.ops.segment_sum(
            forward.reshape(elem_slots * node_slots, 3 * group_size),
            flat_nodes,
            num_segments=node_count + halo_nodes,
        )
        owned_sum = summed[:node_count]
        spilled = summed[node_count:]
        returned = from_behind(spilled, "tiles", 1)
        owned_sum = jnp.concatenate([owned_sum[:halo_nodes] + returned, owned_sum[halo_nodes:]], 0)
        weighted = (obs_weight[:, :, None] * owned_sum.reshape(node_count, 3, group_size)).astype(
            jnp.bfloat16
        )
        weighted = weighted.reshape(node_count, 3 * group_size)
        weighted_rim = from_behind(weighted[:halo_nodes], "tiles", -1)
        node_window = jnp.concatenate([weighted, weighted_rim], 0)
        adjoint_in = node_window[connectivity].reshape(elem_slots, block_order, group_size)
        adjoint_out = jnp.einsum(
            "eji,ejp->eip", blocks, adjoint_in, preferred_element_type=jnp.float32
        )
        partials = jnp.sum(
            friction[:, :, :, None] * adjoint_out.reshape(elem_slots, node_slots, 3, group_size),
            axis=2,
        )
        partials = jnp.where(alive_slots[:, None, None], partials, jnp.float32(0.0))
        basal = jax.ops.segment_sum(
            partials.reshape(elem_slots * node_slots, group_size),
            flat_cells,
            num_segments=cell_count + 2 * rim_cells,
        )
        from_next = from_behind(basal[:rim_cells], "tiles", -1)
        from_prev = from_behind(basal[cell_count + rim_cells :], "tiles", 1)
        middle = basal[rim_cells : cell_count + rim_cells]
        middle = middle + jnp.pad(from_prev, ((0, cell_count - rim_cells), (0, 0)))
        middle = middle + jnp.pad(from_next, ((cell_count - rim_cells, 0), (0, 0)))
        return middle

    parity = jnp.arange(group_size, dtype=jnp.int32) % 2
    same_colour = (cluster_ids % 2)[:, None] == parity[None, :]
    probe_start = jnp.where(same_colour, (2 * sign_bits - 1).astype(jnp.float32), jnp.float32(0.0))
    samples = jnp.where(same_colour, jnp.float32(0.0), hessian(probe_start))
    current = samples
    for power_step in range(POWER):
        squares = lax.psum(jnp.sum(current * current, axis=0), "tiles")
        rms_scale = jnp.sqrt(squares / (cell_count * tile_count) + 1e-06)
        applied = hessian(current / rms_scale)
        if power_step % 2 == 0:
            current = jnp.where(same_colour, applied, jnp.float32(0.0))
        else:
            current = jnp.where(same_colour, jnp.float32(0.0), applied)
    onehot = (cluster_ids[:, None] == jnp.arange(tile_count, dtype=jnp.int32)[None, :]).astype(
        jnp.float32
    )
    column_block = lax.all_gather(current, "probes", axis=1, tiled=True)
    outer = current[:, :, None] * column_block[:, None, :]
    width = column_block.shape[1]
    result = jnp.dot(
        onehot.T, outer.reshape(cell_count, group_size * width), precision=lax.Precision.HIGHEST
    )
    partial_gram = result.reshape(tile_count, group_size, width)
    gram = lax.psum(partial_gram, "tiles")
    return (samples, current, gram)


def solution(mesh):
    in_specs = (
        P("tiles", None, None),
        P("tiles", None),
        P("tiles", None),
        P("tiles", None, None),
        P("tiles"),
        P("tiles", None),
        P("tiles", "probes"),
        P("tiles"),
    )
    out_specs = (P("tiles", "probes"), P("tiles", "probes"), P(None, "probes", None))
    return jax.shard_map(shards, mesh=mesh, in_specs=in_specs, out_specs=out_specs, check_vma=False)
```

profile of v0, /device:TPU:4, one launch (start us, length us, event | category | flops | bytes accessed | tf_op | source)
XLA Modules:
  0.0 1263.8 jit_solution(13736577192659652602)
XLA Ops:
  8.8 3.8 collective-permute-start
  12.6 1.3 collective-permute-start.1
  18.3 10.8 gather_fusion
  30.6 4.5 fusion.2
  35.1 4.1 copy.177
  39.1 5.3 reshape.163
  44.4 23.2 %scatter_custom_fusion = f32[4608,24]{1,0:T(8,128)S(1)} fusion(s32[4096]{0:T(1024)S(1)} %reshape.161, f32[4096,24]{1,0:T(8,128)} %reshape.163, f32[]{:T(128)} %constant.39.clone.1), kind=kCustom, calls=%fused_computation.25 | custom fusion | flops 98304 | bytes 442880 | tf_op jit(solution)/shard_map/scatter-add | solution.py:53
  67.6 4.5 collective-permute-start.2
  72.3 1.4 slice.145
  73.7 2.0 copy.179
  77.7 1.3 collective-permute-start.3
  79.3 4.7 collective-permute-done.3
  84.6 14.9 %gather_fusion.1 = bf16[4096,24]{1,0:T(8,128)(2,1)} fusion(bf16[4608,24]{1,0:T(8,128)(2,1)S(1)} %copy.180, s32[4096]{0:T(1024)S(1)} %broadcast_clamp_fusion), kind=kCustom, calls=%fused_computation.1 | custom fusion | bytes 409600 | tf_op jit(solution)/shard_map/gather | solution.py:68
  99.5 3.7 reshape.101
  103.2 4.6 convolution_bitcast_fusion.2
  107.8 1.4 copy.182
  110.2 22.4 %scatter_custom_fusion.1 = f32[384,8]{1,0:T(8,128)S(1)} fusion(s32[4096]{0:T(1024)S(1)} %reshape.169, f32[4096,8]{1,0:T(8,128)S(1)} %copy.184, f32[]{:T(128)} %constant.39.clone.1), kind=kCustom, calls=%fused_computation.63 | custom fusion | flops 32768 | bytes 12292 | tf_op jit(solution)/shard_map/scatter-add | solution.py:77
  132.7 1.3 collective-permute-start.5
  134.0 5.2 collective-permute-start.4
  140.8 161.9 %psum.21 = f32[8]{0:T(128)S(1)} all-reduce(f32[8]{0:T(128)S(1)} %get-tuple-element.15), channel_id=1, replica_groups=mesh['tiles'=64,'probes'=4] {'tiles'}, use_global_device_ids=true, to_apply=%region_4.5 | all-reduce | flops 8 | bytes 64 | tf_op jit(solution)/shard_map/psum | solution.py:95
  302.8 1.3 collective-permute-start.6
  304.1 1.5 collective-permute-start.7
  305.6 4.0 collective-permute-done.7
  309.8 10.8 gather_fusion.2
  322.1 4.5 fusion.1
  326.6 4.1 copy.191
  330.7 5.3 reshape.179
  335.9 23.2 %scatter_custom_fusion.2 = f32[4608,24]{1,0:T(8,128)S(1)} fusion(s32[4096]{0:T(1024)S(1)} %reshape.161, f32[4096,24]{1,0:T(8,128)} %reshape.179, f32[]{:T(128)} %constant.39.clone.1), kind=kCustom, calls=%fused_computation.23 | custom fusion | flops 98304 | bytes 442880 | tf_op jit(solution)/shard_map/scatter-add | solution.py:53
  359.2 2.4 collective-permute-start.8
  361.6 1.4 slice.155
  362.9 2.0 copy.193
  366.1 1.3 collective-permute-start.9
  367.4 4.8 collective-permute-done.9
  372.7 14.9 %gather_fusion.3 = bf16[4096,24]{1,0:T(8,128)(2,1)} fusion(bf16[4608,24]{1,0:T(8,128)(2,1)S(1)} %copy.194, s32[4096]{0:T(1024)S(1)} %broadcast_clamp_fusion), kind=kCustom, calls=%fused_computation.3 | custom fusion | bytes 409600 | tf_op jit(solution)/shard_map/gather | solution.py:68
  387.6 3.7 reshape.105
  391.4 4.6 convolution_bitcast_fusion.1
  395.9 1.4 copy.196
  398.3 22.4 %scatter_custom_fusion.3 = f32[384,8]{1,0:T(8,128)S(1)} fusion(s32[4096]{0:T(1024)S(1)} %reshape.169, f32[4096,8]{1,0:T(8,128)S(1)} %copy.198, f32[]{:T(128)} %constant.39.clone.1), kind=kCustom, calls=%fused_computation.61 | custom fusion | flops 32768 | bytes 12292 | tf_op jit(solution)/shard_map/scatter-add | solution.py:77
  420.9 1.3 collective-permute-start.11
  422.2 4.5 collective-permute-start.10
  428.2 157.2 %psum.22 = f32[8]{0:T(128)S(1)} all-reduce(f32[8]{0:T(128)S(1)} %multiply_reduce_fusion.3), channel_id=1, replica_groups=mesh['tiles'=64,'probes'=4] {'tiles'}, use_global_device_ids=true, to_apply=%region_9.10 | all-reduce | flops 8 | bytes 64 | tf_op jit(solution)/shard_map/psum | solution.py:95
  585.6 1.3 collective-permute-start.12
  586.9 1.5 collective-permute-start.13
  588.4 4.0 collective-permute-done.13
  592.6 10.8 gather_fusion.4
  604.9 4.5 fusion
  609.4 4.1 copy.205
  613.5 5.3 reshape.195
  618.7 23.2 %scatter_custom_fusion.4 = f32[4608,24]{1,0:T(8,128)S(1)} fusion(s32[4096]{0:T(1024)S(1)} %reshape.161, f32[4096,24]{1,0:T(8,128)} %reshape.195, f32[]{:T(128)} %constant.39.clone.1), kind=kCustom, calls=%fused_computation.21 | custom fusion | flops 98304 | bytes 442880 | tf_op jit(solution)/shard_map/scatter-add | solution.py:53
  642.0 2.4 collective-permute-start.14
  644.4 1.4 slice.165
  645.7 2.0 copy.207
  648.9 1.3 collective-permute-start.15
  650.2 4.8 collective-permute-done.15
  655.5 14.9 %gather_fusion.5 = bf16[4096,24]{1,0:T(8,128)(2,1)} fusion(bf16[4608,24]{1,0:T(8,128)(2,1)S(1)} %copy.208, s32[4096]{0:T(1024)S(1)} %broadcast_clamp_fusion), kind=kCustom, calls=%fused_computation.5 | custom fusion | bytes 409600 | tf_op jit(solution)/shard_map/gather | solution.py:68
  670.4 3.7 reshape.109
  674.1 4.6 convolution_bitcast_fusion
  678.7 1.4 copy.210
  681.1 22.4 %scatter_custom_fusion.5 = f32[384,8]{1,0:T(8,128)S(1)} fusion(s32[4096]{0:T(1024)S(1)} %reshape.169, f32[4096,8]{1,0:T(8,128)S(1)} %copy.212, f32[]{:T(128)} %constant.39.clone.1), kind=kCustom, calls=%fused_computation.59 | custom fusion | flops 32768 | bytes 12292 | tf_op jit(solution)/shard_map/scatter-add | solution.py:77
  703.7 1.3 collective-permute-start.17
  705.0 4.5 collective-permute-start.16
  710.9 6.7 all_gather.3
  718.5 536.8 %all-reduce.8.cloned.1.call-done = f32[64,8,32]{0,2,1:T(8,128)} async-done(((f32[64,8,32]{0,2,1:T(8,128)}), f32[64,8,32]{0,2,1:T(8,128)}) %all-reduce.8.cloned.1.call-update) | async-done | bytes 65552 | tf_op jit(solution)/shard_map/psum | solution.py:112
  1255.3 1.6 copy.230
  (121 shorter events, 25.5 us)
Async XLA Ops:
  7.2 1248.2 %all-reduce.8.cloned.1.call-start = ((), (), s32[]{:S(2)}) async-start(), calls=%async_computation | async-start | bytes 262144 | tf_op jit(solution)/shard_map/psum | solution.py:112
  8.8 8.5 collective-permute-start
  12.6 5.5 collective-permute-start.1
  44.4 27.8 %copy-start.1 = (s32[64,64]{1,0:T(8,128)S(1)}, s32[64,64]{1,0:T(8,128)}, u32[]{:S(2)}) copy-start(s32[64,64]{1,0:T(8,128)} %param.9) | copy-start | bytes 49156
  44.4 27.8 %copy-start = (f32[4096,3]{0,1:T(4,128)S(1)}, f32[4096,3]{0,1:T(4,128)}, u32[]{:S(2)}) copy-start(f32[4096,3]{0,1:T(4,128)} %param.13) | copy-start | bytes 147460
  67.6 8.9 collective-permute-start.2
  73.7 5.4 copy-start.2
  77.7 6.3 collective-permute-start.3
  132.7 6.6 collective-permute-start.5
  134.0 6.5 collective-permute-start.4
  140.7 179.9 %copy-start.4 = (f32[256,8]{0,1:T(8,128)}, f32[256,8]{0,1:T(8,128)S(1)}, u32[]{:S(2)}) copy-start(f32[256,8]{0,1:T(8,128)S(1)} %get-tuple-element.35) | copy-start | bytes 24580
  302.8 2.8 collective-permute-start.6
  304.1 5.5 collective-permute-start.7
  359.2 5.7 collective-permute-start.8
  366.1 6.1 collective-permute-start.9
  420.9 5.9 collective-permute-start.11
  422.2 5.9 collective-permute-start.10
  585.6 2.8 collective-permute-start.12
  586.9 5.5 collective-permute-start.13
  642.0 5.7 collective-permute-start.14
  648.9 6.1 collective-permute-start.15
  680.2 37.4 %copy-start.5 = (s32[256]{0:T(256)S(1)}, s32[256]{0:T(256)}, u32[]{:S(2)}) copy-start(s32[256]{0:T(256)} %param.15) | copy-start | bytes 3076
  703.7 5.9 collective-permute-start.17
  705.0 5.9 collective-permute-start.16
  710.9 546.0 %copy-start.3 = (f32[256,8]{0,1:T(8,128)}, f32[256,8]{0,1:T(8,128)S(1)}, u32[]{:S(2)}) copy-start(f32[256,8]{0,1:T(8,128)S(1)} %compare_select_fusion.2) | copy-start | bytes 24580
Sparse Core Ops, SparseCore 0:
  718.7 536.6 all-reduce.7
where the time goes:
time: 1270 us; the launch traced here: 1260 us
  waiting for transfers between devices  564 us (44%)
  blocking collectives  326 us (26%)
  other arithmetic  144 us (11%)
  local copies, waits for them, and re-layouts  144 us (11%)
  starting transfers between devices  42.1 us (3%)
  matrix products  28.1 us (2%)
  between operations  15.4 us (1%)
    psum x1, waiting for transfers between devices, shards(): gram = lax.psum(partial_gram, 'tiles')  537 us
    psum x2, blocking collectives, shards(): squares = lax.psum(jnp.sum(current * current, axis=0), 'tiles')  319 us
    scatter-add x3, other arithmetic, hessian(): jax.ops.segment_sum(forward.reshape(elem_slots * node_slots, 3 * group_si...  69.7 us
    scatter-add x3, other arithmetic, hessian(): jax.ops.segment_sum(partials.reshape(elem_slots * node_slots, group_size)...  67.2 us
    gather x3, local copies, waits for them, and re-layouts, hessian(): node_window[connectivity].reshape(elem_slots, block_order, group_size)  44.7 us
    gather x6, local copies, waits for them, and re-layouts, hessian(): picked = window[basal_map]  35.6 us
    ppermute x12, starting transfers between devices, from_behind(): return lax.ppermute(block, axis, route)  31.4 us
  transfers between devices with their start and end apart: 19, of which 11 were waited for; matrix products, arithmetic and copies ran while one was open for 1% of the time, Pallas kernels for 0%

commit v1 on v0

--- a/solution.py
+++ b/solution.py
@@ -6,6 +6,11 @@
 HALO = 512
 POWER = 2
 RIM = 64
+
+
+def add_all(array, axis):
+    parts = lax.all_gather(array, axis)
+    return jnp.sum(parts, axis=0)
 
 
 def padded(x, sides, width):
@@ -92,7 +97,7 @@
     samples = jnp.where(same_colour, jnp.float32(0.0), hessian(probe_start))
     current = samples
     for power_step in range(POWER):
-        squares = lax.psum(jnp.sum(current * current, axis=0), "tiles")
+        squares = add_all(jnp.sum(current * current, axis=0), "tiles")
         rms_scale = jnp.sqrt(squares / (cell_count * tile_count) + 1e-06)
         applied = hessian(current / rms_scale)
         if power_step % 2 == 0:

time: 1270 us -> 1260 us (level)
    psum x2 -> x0, blocking collectives: 319 us -> none  [shards(): squares = lax.psum(jnp.sum(current * current, axis=0), 'tiles')]
    unnamed x0 -> x2, blocking collectives: none -> 309 us
where the time goes in v1:
time: 1260 us
  waiting for transfers between devices  570 us (45%)
  blocking collectives  316 us (25%)
  local copies, waits for them, and re-layouts  145 us (12%)
  other arithmetic  144 us (11%)
  starting transfers between devices  42.6 us (3%)
  matrix products  28.1 us (2%)
  between operations  16.1 us (1%)
    psum x1, waiting for transfers between devices, shards(): gram = lax.psum(partial_gram, 'tiles')  534 us
    unnamed x2, blocking collectives  309 us
    scatter-add x3, other arithmetic, hessian(): jax.ops.segment_sum(forward.reshape(elem_slots * node_slots, 3 * group_si...  69.7 us
    scatter-add x3, other arithmetic, hessian(): jax.ops.segment_sum(partials.reshape(elem_slots * node_slots, group_size)...  67.2 us
    gather x3, local copies, waits for them, and re-layouts, hessian(): node_window[connectivity].reshape(elem_slots, block_order, group_size)  44.7 us
    gather x6, local copies, waits for them, and re-layouts, hessian(): picked = window[basal_map]  35.6 us
    ppermute x12, starting transfers between devices, from_behind(): return lax.ppermute(block, axis, route)  29.7 us
    ppermute x12, waiting for transfers between devices, from_behind(): return lax.ppermute(block, axis, route)  27 us
  transfers between devices with their start and end apart: 19, of which 11 were waited for; matrix products, arithmetic and copies ran while one was open for 1% of the time, Pallas kernels for 0%

profile of v1, /device:TPU:4, one launch (start us, length us, event | category | flops | bytes accessed | tf_op | source)
XLA Modules:
  0.0 1261.8 jit_solution(2645886326257581653)
XLA Ops:
  8.8 3.8 collective-permute-start
  12.6 1.3 collective-permute-start.1
  18.3 10.8 gather_fusion
  30.6 4.5 fusion.2
  35.1 4.1 copy.177
  39.1 5.3 reshape.171
  44.4 23.2 %scatter_custom_fusion = f32[4608,24]{1,0:T(8,128)S(1)} fusion(s32[4096]{0:T(1024)S(1)} %reshape.169, f32[4096,24]{1,0:T(8,128)} %reshape.171, f32[]{:T(128)} %constant.39.clone.1), kind=kCustom, calls=%fused_computation.25 | custom fusion | flops 98304 | bytes 442880 | tf_op jit(solution)/shard_map/scatter-add | solution.py:58
  67.6 4.5 collective-permute-start.2
  72.3 1.4 slice.145
  73.7 2.0 copy.179
  77.8 1.3 collective-permute-start.3
  79.3 4.7 collective-permute-done.3
  84.6 14.9 %gather_fusion.1 = bf16[4096,24]{1,0:T(8,128)(2,1)} fusion(bf16[4608,24]{1,0:T(8,128)(2,1)S(1)} %copy.180, s32[4096]{0:T(1024)S(1)} %broadcast_clamp_fusion), kind=kCustom, calls=%fused_computation.1 | custom fusion | bytes 409600 | tf_op jit(solution)/shard_map/gather | solution.py:73
  99.5 3.7 reshape.109
  103.2 4.6 convolution_bitcast_fusion.2
  107.8 1.4 copy.182
  110.2 22.4 %scatter_custom_fusion.1 = f32[384,8]{1,0:T(8,128)S(1)} fusion(s32[4096]{0:T(1024)S(1)} %reshape.177, f32[4096,8]{1,0:T(8,128)S(1)} %copy.184, f32[]{:T(128)} %constant.39.clone.1), kind=kCustom, calls=%fused_computation.63 | custom fusion | flops 32768 | bytes 12292 | tf_op jit(solution)/shard_map/scatter-add | solution.py:82
  132.7 4.6 collective-permute-start.4
  137.3 1.3 collective-permute-start.5
  140.0 3.6 collective-permute-done.5
  144.0 156.7 %all-reduce.6 = f32[512]{0:T(512)S(1)} all-reduce(f32[512]{0:T(512)S(1)} %dynamic-update-slice), channel_id=2, replica_groups=mesh['tiles'=64,'probes'=4] {'tiles'}, use_global_device_ids=true, to_apply=%add.6 | all-reduce | flops 512 | bytes 4096
  302.3 1.3 collective-permute-start.7
  303.6 4.2 collective-permute-done.7
  308.0 10.8 gather_fusion.2
  320.3 4.5 fusion.1
  324.8 4.1 copy.191
  328.9 5.3 reshape.187
  334.1 23.2 %scatter_custom_fusion.2 = f32[4608,24]{1,0:T(8,128)S(1)} fusion(s32[4096]{0:T(1024)S(1)} %reshape.169, f32[4096,24]{1,0:T(8,128)} %reshape.187, f32[]{:T(128)} %constant.39.clone.1), kind=kCustom, calls=%fused_computation.23 | custom fusion | flops 98304 | bytes 442880 | tf_op jit(solution)/shard_map/scatter-add | solution.py:58
  357.4 2.4 collective-permute-start.8
  359.8 1.4 slice.155
  361.1 2.0 copy.193
  364.3 1.3 collective-permute-start.9
  365.6 4.8 collective-permute-done.9
  370.9 14.9 %gather_fusion.3 = bf16[4096,24]{1,0:T(8,128)(2,1)} fusion(bf16[4608,24]{1,0:T(8,128)(2,1)S(1)} %copy.194, s32[4096]{0:T(1024)S(1)} %broadcast_clamp_fusion), kind=kCustom, calls=%fused_computation.3 | custom fusion | bytes 409600 | tf_op jit(solution)/shard_map/gather | solution.py:73
  385.8 3.7 reshape.113
  389.5 4.6 convolution_bitcast_fusion.1
  394.1 1.4 copy.196
  396.5 22.4 %scatter_custom_fusion.3 = f32[384,8]{1,0:T(8,128)S(1)} fusion(s32[4096]{0:T(1024)S(1)} %reshape.177, f32[4096,8]{1,0:T(8,128)S(1)} %copy.198, f32[]{:T(128)} %constant.39.clone.1), kind=kCustom, calls=%fused_computation.61 | custom fusion | flops 32768 | bytes 12292 | tf_op jit(solution)/shard_map/scatter-add | solution.py:82
  419.0 3.9 collective-permute-start.10
  424.4 4.1 collective-permute-done.11
  428.9 152.7 %all-reduce.7 = f32[512]{0:T(512)S(1)} all-reduce(f32[512]{0:T(512)S(1)} %dynamic-update-slice.1), channel_id=3, replica_groups=mesh['tiles'=64,'probes'=4] {'tiles'}, use_global_device_ids=true, to_apply=%add.7 | all-reduce | flops 512 | bytes 4096
  581.9 3.6 collective-permute-start.12
  585.5 1.5 collective-permute-start.13
  587.1 4.0 collective-permute-done.13
  591.2 10.8 gather_fusion.4
  603.6 4.5 fusion
  608.0 4.1 copy.205
  612.1 5.3 reshape.203
  617.3 23.2 %scatter_custom_fusion.4 = f32[4608,24]{1,0:T(8,128)S(1)} fusion(s32[4096]{0:T(1024)S(1)} %reshape.169, f32[4096,24]{1,0:T(8,128)} %reshape.203, f32[]{:T(128)} %constant.39.clone.1), kind=kCustom, calls=%fused_computation.21 | custom fusion | flops 98304 | bytes 442880 | tf_op jit(solution)/shard_map/scatter-add | solution.py:58
  640.6 2.6 collective-permute-start.14
  643.2 1.4 slice.165
  644.6 2.0 copy.207
  647.8 1.3 collective-permute-start.15
  649.1 4.8 collective-permute-done.15
  654.4 14.9 %gather_fusion.5 = bf16[4096,24]{1,0:T(8,128)(2,1)} fusion(bf16[4608,24]{1,0:T(8,128)(2,1)S(1)} %copy.208, s32[4096]{0:T(1024)S(1)} %broadcast_clamp_fusion), kind=kCustom, calls=%fused_computation.5 | custom fusion | bytes 409600 | tf_op jit(solution)/shard_map/gather | solution.py:73
  669.3 3.7 reshape.117
  673.0 4.6 convolution_bitcast_fusion
  677.6 1.4 copy.210
  680.0 22.4 %scatter_custom_fusion.5 = f32[384,8]{1,0:T(8,128)S(1)} fusion(s32[4096]{0:T(1024)S(1)} %reshape.177, f32[4096,8]{1,0:T(8,128)S(1)} %copy.212, f32[]{:T(128)} %constant.39.clone.1), kind=kCustom, calls=%fused_computation.59 | custom fusion | flops 32768 | bytes 12292 | tf_op jit(solution)/shard_map/scatter-add | solution.py:82
  702.5 3.9 collective-permute-start.16
  707.9 4.1 collective-permute-done.17
  712.1 6.7 all_gather.19
  719.7 533.7 %all-reduce.10.cloned.1.call-done = f32[64,8,32]{0,2,1:T(8,128)} async-done(((f32[64,8,32]{0,2,1:T(8,128)}), f32[64,8,32]{0,2,1:T(8,128)}) %all-reduce.10.cloned.1.call-update) | async-done | bytes 65552 | tf_op jit(solution)/shard_map/psum | solution.py:117
  1253.4 1.6 copy.240
  (132 shorter events, 27.0 us)
Async XLA Ops:
  7.2 1246.2 %all-reduce.10.cloned.1.call-start = ((), (), s32[]{:S(2)}) async-start(), calls=%async_computation | async-start | bytes 262144 | tf_op jit(solution)/shard_map/psum | solution.py:117
  8.8 8.5 collective-permute-start
  12.6 5.5 collective-permute-start.1
  44.4 27.8 %copy-start.1 = (s32[64,64]{1,0:T(8,128)S(1)}, s32[64,64]{1,0:T(8,128)}, u32[]{:S(2)}) copy-start(s32[64,64]{1,0:T(8,128)} %param.9) | copy-start | bytes 49156
  44.4 27.8 %copy-start = (f32[4096,3]{0,1:T(4,128)S(1)}, f32[4096,3]{0,1:T(4,128)}, u32[]{:S(2)}) copy-start(f32[4096,3]{0,1:T(4,128)} %param.13) | copy-start | bytes 147460
  67.6 8.9 collective-permute-start.2
  73.7 5.4 copy-start.2
  77.8 6.3 collective-permute-start.3
  109.2 29.5 %copy-start.6 = (u32[256]{0:T(256)S(1)}, u32[256]{0:T(256)}, u32[]{:S(2)}) copy-start(u32[256]{0:T(256)} %constant.60) | copy-start | bytes 3076
  132.7 7.3 collective-permute-start.4
  137.3 6.2 collective-permute-start.5
  143.7 175.1 %copy-start.4 = (f32[256,8]{0,1:T(8,128)}, f32[256,8]{0,1:T(8,128)S(1)}, u32[]{:S(2)}) copy-start(f32[256,8]{0,1:T(8,128)S(1)} %get-tuple-element.35) | copy-start | bytes 24580
  301.0 2.6 collective-permute-start.6
  302.3 5.5 collective-permute-start.7
  357.4 5.7 collective-permute-start.8
  364.3 6.1 collective-permute-start.9
  419.0 5.4 collective-permute-start.10
  423.0 5.5 collective-permute-start.11
  581.9 5.2 collective-permute-start.12
  585.5 5.5 collective-permute-start.13
  640.6 6.0 collective-permute-start.14
  647.8 6.1 collective-permute-start.15
  679.1 39.7 %copy-start.5 = (s32[256]{0:T(256)S(1)}, s32[256]{0:T(256)}, u32[]{:S(2)}) copy-start(s32[256]{0:T(256)} %param.15) | copy-start | bytes 3076
  702.5 5.4 collective-permute-start.16
  706.5 5.5 collective-permute-start.17
  712.0 542.9 %copy-start.3 = (f32[256,8]{0,1:T(8,128)}, f32[256,8]{0,1:T(8,128)S(1)}, u32[]{:S(2)}) copy-start(f32[256,8]{0,1:T(8,128)S(1)} %compare_select_fusion.2) | copy-start | bytes 24580
Sparse Core Ops, SparseCore 0:
  719.8 533.5 all-reduce.9
